TPU v7x, 512 devices: a whole 4x8x8 slice. The times are simulated.
512 devices in a mesh: row: 16 (over z, core), col: 32 (over y, x).
Axes of the slice: x: 4, y: 8, z: 8, core: 2. Of those that a mesh axis runs over, the one named last changes fastest.
Arguments:
- tokens: bfloat16 [4096, 2560], P('row', 'col'), may hold values from -6 to 6
- w_down: bfloat16 [2560, 1056], P('col'), may hold values from -0.125 to 0.125
- q_gain: float32 [768], replicated, may hold values from 0.1 to 1.9
- kv_gain: float32 [256], replicated, may hold values from 0.1 to 1.9
- w_q_up: bfloat16 [768, 3072], P(None, 'col'), may hold values from -8.8767604 to 8.8767604
- w_kv_up: bfloat16 [256, 4096], replicated, may hold values from -0.375 to 0.375
- w_out: bfloat16 [2048, 2560], P('col'), may hold values from -0.75 to 0.75
- latent_cache: bfloat16 [16, 8192, 288], P('row', 'col'), may hold values from -6 to 6
- cache_len: int32 [16], replicated, may hold values from 1 to 8192, as said below
- new_len: int32 [16], replicated, may hold values from 1 to 256, as said below
- page_table: int32 [16, 128], replicated, may hold values from 0 to 127, each once within a row
- home_slot: int32 [16], replicated, may hold values from 0 to 15, each once
Outputs:
- output: bfloat16 [4096, 2560], P('row', 'col')
Inputs may be any that keep to these rules, and one draw needn't show every extreme that they name: `cache_len`: some slot has exactly 8192 cached tokens; about half the slots hold at most 1024, the others at least 7168. `new_len`: some request has exactly 256 real new tokens.
All inputs are finite; a program needn't handle non-finite values.
Results may differ from a plain program's by a relative error of at most 0.023.
Values may be sent and summed in bfloat16 or wider, within the bound.
A program may use at most 64 MiB of HBM per device.

v0:
```python
import math
import jax
import jax.numpy as jnp
from jax import lax
from jax.sharding import PartitionSpec as P

NOPE = 64
ROPE = 32
VDIM = 64
epsilon = 1e-05


def rms_scale(values, gain):
    return values * lax.rsqrt(jnp.mean(values * values, axis=-1, keepdims=True) + epsilon) * gain


def angle_tables(positions, width):
    half_dim = width // 2
    frequency = 10000.0 ** (-2.0 * jnp.arange(half_dim, dtype=jnp.float32) / width)
    angles = positions.astype(jnp.float32)[:, None] * frequency[None, :]
    return (jnp.cos(angles), jnp.sin(angles))


def rotary(values, cosine, sine_table):
    half_dim = values.shape[-1] // 2
    first_half = values[..., :half_dim]
    second_half = values[..., half_dim:]
    return jnp.concatenate(
        [
            first_half * cosine - second_half * sine_table,
            second_half * cosine + first_half * sine_table,
        ],
        -1,
    )


def body(
    tokens,
    w_down,
    q_gain,
    kv_gain,
    w_q_up,
    w_kv_up,
    w_out,
    latent_cache,
    cache_len,
    new_len,
    page_table,
    home_slot,
):
    columns = lax.axis_size("col")
    column_id = lax.axis_index("col")
    row_id = lax.axis_index("row")
    group_rows = tokens.shape[0]
    own_rows = group_rows // columns
    q_width = q_gain.shape[0]
    kv_width = kv_gain.shape[0]
    slot_index = home_slot[row_id]
    cached_count = cache_len[slot_index]
    live_count = new_len[row_id]
    combined = lax.psum_scatter(
        jnp.dot(tokens, w_down, preferred_element_type=jnp.float32),
        "col",
        scatter_dimension=0,
        tiled=True,
    )
    own_position = cached_count + column_id * own_rows + jnp.arange(own_rows, dtype=jnp.int32)
    own_cos, own_sin = angle_tables(own_position, ROPE)
    query_latent = rms_scale(combined[:, :q_width], q_gain).astype(jnp.bfloat16)
    new_latent = rms_scale(combined[:, q_width : q_width + kv_width], kv_gain).astype(jnp.bfloat16)
    new_rope = rotary(combined[:, q_width + kv_width :], own_cos, own_sin).astype(jnp.bfloat16)
    new_rows = jnp.concatenate([new_latent, new_rope], 1)
    projected = jnp.dot(
        lax.all_gather(query_latent, "col", axis=0, tiled=True),
        w_q_up,
        preferred_element_type=jnp.float32,
    )
    query_cos, query_sin = angle_tables(
        cached_count + jnp.arange(group_rows, dtype=jnp.int32), ROPE
    )
    queries = jnp.concatenate(
        [projected[:, :NOPE], rotary(projected[:, NOPE:], query_cos, query_sin)], 1
    ).astype(jnp.bfloat16)
    segment = lax.all_gather(latent_cache, "row", axis=0, tiled=True)
    matches = jnp.arange(segment.shape[0], dtype=jnp.int32) == slot_index
    own_cache = jnp.sum(
        jnp.where(matches[:, None, None], segment.astype(jnp.float32), 0.0), 0
    ).astype(jnp.bfloat16)
    head_width = NOPE + VDIM
    head_weight = lax.dynamic_slice_in_dim(w_kv_up, column_id * head_width, head_width, 1)

    def expand(latents):
        lifted = jnp.dot(
            latents[:, :kv_width], head_weight, preferred_element_type=jnp.float32
        ).astype(jnp.bfloat16)
        return (jnp.concatenate([lifted[:, :NOPE], latents[:, kv_width:]], 1), lifted[:, NOPE:])

    cache_latents, fresh_latents = (
        lax.all_gather(own_cache, "col", axis=0, tiled=True),
        lax.all_gather(new_rows, "col", axis=0, tiled=True),
    )
    cache_keys, cache_values = expand(cache_latents)
    fresh_keys, fresh_values = expand(fresh_latents)
    key_total = cache_keys.shape[0]
    page_row = page_table[slot_index]
    page_count = page_row.shape[0]
    page_size = key_total // page_count
    block_size = min(512, key_total)
    offsets = jnp.arange(page_size, dtype=jnp.int32)
    page_ids = jnp.arange(page_count, dtype=jnp.int32)
    logical_page = jnp.sum(
        page_ids[:, None] * (page_row[:, None] == page_ids[None, :]).astype(jnp.int32), 0
    )
    cached_visible = (logical_page[:, None] * page_size + offsets[None, :]).reshape(
        key_total
    ) < cached_count
    block_limit = key_total // block_size
    score_scale = 1.0 / math.sqrt(NOPE + ROPE)
    query_index = jnp.arange(group_rows, dtype=jnp.int32)[:, None]
    key_index = jnp.arange(group_rows, dtype=jnp.int32)[None, :]
    fresh_visible = (key_index <= query_index) & (key_index < live_count)
    fresh_scores = (
        jnp.einsum("qd,kd->qk", queries, fresh_keys, preferred_element_type=jnp.float32)
        * score_scale
    )
    fresh_scores = jnp.where(fresh_visible, fresh_scores, -jnp.inf)
    first_peak = jnp.max(fresh_scores, 1)
    fresh_exponent = jnp.exp(fresh_scores - first_peak[:, None])
    start_state = (
        first_peak,
        jnp.sum(fresh_exponent, 1),
        jnp.dot(
            fresh_exponent.astype(jnp.bfloat16), fresh_values, preferred_element_type=jnp.float32
        ),
    )

    def accumulate(block_id, running):
        row_peak, row_total, summed = running
        key_block = lax.dynamic_slice_in_dim(cache_keys, block_id * block_size, block_size, 0)
        mask_block = lax.dynamic_slice_in_dim(cached_visible, block_id * block_size, block_size, 0)
        value_block = lax.dynamic_slice_in_dim(cache_values, block_id * block_size, block_size, 0)
        raw_scores = (
            jnp.einsum("qd,kd->qk", queries, key_block, preferred_element_type=jnp.float32)
            * score_scale
        )
        raw_scores = jnp.where(mask_block[None, :], raw_scores, -jnp.inf)
        next_peak = jnp.maximum(row_peak, jnp.max(raw_scores, 1))
        factor = jnp.exp(row_peak - next_peak)
        exponent = jnp.exp(raw_scores - next_peak[:, None])
        next_total = row_total * factor + jnp.sum(exponent, 1)
        next_summed = summed * factor[:, None] + jnp.dot(
            exponent.astype(jnp.bfloat16), value_block, preferred_element_type=jnp.float32
        )
        return (next_peak, next_total, next_summed)

    row_peak, row_total, summed = lax.fori_loop(0, block_limit, accumulate, start_state)
    attended = (summed / row_total[:, None]).astype(jnp.bfloat16)
    live_rows = jnp.arange(group_rows, dtype=jnp.int32) < live_count
    attended = jnp.where(live_rows[:, None], attended, jnp.zeros_like(attended))
    summed_out = lax.psum_scatter(
        lax.dot_general(
            w_out, attended, (((0,), (1,)), ((), ())), preferred_element_type=jnp.float32
        ).astype(jnp.bfloat16),
        "col",
        scatter_dimension=0,
        tiled=True,
    ).astype(jnp.float32)
    result = summed_out.T.astype(jnp.bfloat16)
    return result


def solution(mesh):
    return jax.shard_map(
        body,
        mesh=mesh,
        in_specs=(
            P("row", "col"),
            P("col", None),
            P(),
            P(),
            P(None, "col"),
            P(),
            P("col", None),
            P("row", "col", None),
            P(),
            P(),
            P(),
            P(),
        ),
        out_specs=P("row", "col"),
        check_vma=False,
    )
```

profile of v0, /device:TPU:16, one launch (start us, length us, event | category | flops | bytes accessed | tf_op | source)
XLA Modules:
  0.0 535.3 jit_solution(15060410855748943424)
XLA Ops:
  8.1 2.3 fusion.51
  11.9 46.3 %all-gather.3.cloned.1.call-done = bf16[16,256,288]{1,2,0:T(8,128)(2,1)} async-done(((bf16[1,256,288]{1,2,0:T(8,128)(2,1)}), bf16[16,256,288]{1,2,0:T(8,128)(2,1)}) %all-gather.3.cloned.1.call-update) | async-done | bytes 2359312 | tf_op jit(solution)/shard_map/all_gather | solution.py:84
  58.2 2.9 select_reduce_fusion
  66.8 1.3 dynamic-slice
  70.1 106.5 %all-reduce.3.cloned.1.call-done = f32[256,1056]{1,0:T(8,128)} async-done(((f32[256,1056]{1,0:T(8,128)}), f32[256,1056]{1,0:T(8,128)}) %all-reduce.3.cloned.1.call-update) | async-done | bytes 1081360
  176.6 0.9 multiply_reduce_fusion.1
  177.5 0.9 fusion.41
  179.2 44.2 %all_gather.13 = bf16[256,288]{1,0:T(8,128)(2,1)S(1)} all-gather(bf16[8,288]{1,0:T(8,128)(2,1)S(1)} %pad_maximum_fusion.2), channel_id=1, replica_groups=mesh['row'=16,'col'=32] {'col'}, dimensions={0}, use_global_device_ids=true | all-gather | bytes 152064 | tf_op jit(solution)/shard_map/all_gather | solution.py:100
  225.4 46.8 %all_gather.12 = bf16[256,768]{1,0:T(8,128)(2,1)S(1)} all-gather(bf16[8,768]{1,0:T(8,128)(2,1)S(1)} %multiply_convert_fusion), channel_id=1, replica_groups=mesh['row'=16,'col'=32] {'col'}, dimensions={0}, use_global_device_ids=true | all-gather | bytes 405504 | tf_op jit(solution)/shard_map/all_gather | solution.py:74
  273.3 3.0 convolution_convert_fusion
  276.4 0.9 slice-done
  277.3 1.3 pad_maximum_fusion
  278.6 26.9 %while.17 = (s32[]{:T(128)}, f32[256]{0:T(256)S(1)}, f32[256]{0:T(256)S(1)}, f32[256,64]{0,1:T(8,128)S(1)}, pred[8192]{0:T(1024)(128)(4,1)S(1)}, /*index=5*/bf16...) while((s32[]{:T(128)}, f32[256]{0:T(256)S(1)}, ...), condition=%wide.region_10.11_spmd, body=%wide.region_7.10_spmd.sunk | while | flops 42893828 | bytes 1935023 | solution.py:156
  278.6 1.2 fusion.67
  280.3 1.2 fusion.67
  282.0 1.2 fusion.67
  283.7 1.2 fusion.67
  285.4 1.2 fusion.67
  287.1 1.2 fusion.67
  288.7 1.2 fusion.67
  290.4 1.2 fusion.67
  292.1 1.2 fusion.67
  293.8 1.2 fusion.67
  295.5 1.2 fusion.67
  297.2 1.2 fusion.67
  298.8 1.2 fusion.67
  300.5 1.2 fusion.67
  302.2 1.2 fusion.67
  303.9 1.2 fusion.67
  305.5 1.5 fusion.10
  307.0 1.5 copy.43
  308.5 219.2 %reduce-scatter.4.cloned.1.call-done = bf16[80,256]{1,0:T(8,128)(2,1)} async-done(((bf16[2560,256]{1,0:T(8,128)(2,1)}), bf16[80,256]{1,0:T(8,128)(2,1)}) %reduce-scatter.4.cloned.1.call-update) | async-done | bytes 40976
  (152 shorter events, 18.0 us)
Async XLA Ops:
  7.4 216.1 %copy-start = (bf16[256,4096]{1,0:T(8,128)(2,1)S(1)}, bf16[256,4096]{1,0:T(8,128)(2,1)}, u32[]{:S(2)}) copy-start(bf16[256,4096]{1,0:T(8,128)(2,1)} %param.19) | copy-start | bytes 6291460
  7.4 3.2 copy-start.4
  7.4 50.8 %all-gather.3.cloned.1.call-start = ((), (), s32[]{:S(2)}) async-start(), calls=%async_computation.1 | async-start | bytes 2506752 | tf_op jit(solution)/shard_map/all_gather | solution.py:84
  8.1 168.5 %all-reduce.3.cloned.1.call-start = ((), (), s32[]{:S(2)}) async-start(), calls=%async_computation.4 | async-start | bytes 2359296
  10.5 52.0 %copy-start.5 = (s32[16]{0:T(128)S(1)}, s32[16]{0:T(128)}, u32[]{:S(2)}) copy-start(s32[16]{0:T(128)} %param.23) | copy-start | bytes 196
  10.5 53.4 %copy-start.6 = (s32[16]{0:T(128)S(1)}, s32[16]{0:T(128)}, u32[]{:S(2)}) copy-start(s32[16]{0:T(128)} %param.22) | copy-start | bytes 196
  10.5 167.9 %copy-start.3 = (f32[256]{0:T(256)S(1)}, f32[256]{0:T(256)}, u32[]{:S(2)}) copy-start(f32[256]{0:T(256)} %param.17) | copy-start | bytes 3076
  10.5 214.1 %copy-start.2 = (f32[768]{0:T(1024)S(1)}, f32[768]{0:T(1024)}, u32[]{:S(2)}) copy-start(f32[768]{0:T(1024)} %param.16) | copy-start | bytes 9220
  10.5 261.7 %copy-start.1 = (bf16[768,96]{0,1:T(8,128)(2,1)S(1)}, bf16[768,96]{0,1:T(8,128)(2,1)}, u32[]{:S(2)}) copy-start(bf16[768,96]{0,1:T(8,128)(2,1)} %param.18) | copy-start | bytes 442372
  10.5 262.8 %all-gather.5.cloned.1.call-start = ((), (), s32[]{:S(2)}) async-start(), calls=%async_computation.2 | async-start | bytes 4866048 | tf_op jit(solution)/shard_map/all_gather | solution.py:99
  61.1 466.6 %reduce-scatter.4.cloned.1.call-start = ((), (), s32[]{:S(2)}) async-start(), calls=%async_computation.3 | async-start | bytes 1351680
  276.3 1.0 slice-start
Sparse Core Ops, SparseCore 0:
  10.3 47.8 all-gather.2
Sparse Core Ops, SparseCore 1:
  12.0 164.5 all-reduce.2
  179.5 89.1 all-gather.4
  308.6 219.1 reduce-scatter.3
where the time goes:
time: 536 us; the launch traced here: 535 us
  waiting for transfers between devices  373 us (70%)
  blocking collectives  91 us (17%)
  matrix products  30.2 us (6%)
  between operations  18.6 us (3%)
  other arithmetic  13.9 us (3%)
  local copies, waits for them, and re-layouts  8.05 us (2%)
    unnamed x6, waiting for transfers between devices  326 us
    all_gather x1, blocking collectives, body(): lax.all_gather(query_latent, 'col', axis=0, tiled=True)  46.8 us
    all_gather x1, waiting for transfers between devices, body(): segment = lax.all_gather(latent_cache, 'row', axis=0, tiled=True)  46.3 us
    all_gather x1, blocking collectives, body(): lax.all_gather(new_rows, 'col', axis=0, tiled=True)  44.2 us
    dot_general x16, matrix products, accumulate(): jnp.einsum('qd,kd->qk', queries, key_block, preferred_element_type=jnp.fl...  18.8 us
  transfers between devices with their start and end apart: 4, of which 3 were waited for; matrix products, arithmetic and copies ran while one was open for 3% of the time, Pallas kernels for 0%

commit v1 on v0

--- a/solution.py
+++ b/solution.py
@@ -81,7 +81,12 @@
     queries = jnp.concatenate(
         [projected[:, :NOPE], rotary(projected[:, NOPE:], query_cos, query_sin)], 1
     ).astype(jnp.bfloat16)
-    segment = lax.all_gather(latent_cache, "row", axis=0, tiled=True)
+    ring = [latent_cache]
+    for hop in range(15):
+        ring.append(lax.ppermute(ring[-1], "row", [(dev, (dev + 1) % 16) for dev in range(16)]))
+    segment = jnp.roll(
+        jnp.concatenate(ring[::-1], axis=0), (lax.axis_index("row") + 1) * ring[0].shape[0], axis=0
+    )
     matches = jnp.arange(segment.shape[0], dtype=jnp.int32) == slot_index
     own_cache = jnp.sum(
         jnp.where(matches[:, None, None], segment.astype(jnp.float32), 0.0), 0

time: 536 us -> 620 us (1.16)
  waiting for transfers between devices: 373 us -> 445 us
  local copies, waits for them, and re-layouts: 8.05 us -> 20.6 us
    ppermute x0 -> x15, waiting for transfers between devices: none -> 88.3 us  [body(): lax.ppermute(ring[-1], 'row', [(dev, (dev + 1) % 16) for dev in range(16)])]
    all_gather x1 -> x0, waiting for transfers between devices: 46.3 us -> none  [body(): segment = lax.all_gather(latent_cache, 'row', axis=0, tiled=True)]
    unnamed x6 -> x5, waiting for transfers between devices: 326 us -> 357 us
    unnamed x17 -> x66, local copies, waits for them, and re-layouts: 2.84 us -> 14.7 us
  transfers between devices with their start and end apart: 4 -> 18, of which waited for: 3 -> 17; matrix products, arithmetic and copies ran while one was open for 3% -> 4% of each run, Pallas kernels for 0% -> 0%
where the time goes in v1:
time: 620 us; the launch traced here: 618 us
  waiting for transfers between devices  445 us (72%)
  blocking collectives  90.9 us (15%)
  matrix products  31.1 us (5%)
  local copies, waits for them, and re-layouts  20.6 us (3%)
  between operations  16.9 us (3%)
  other arithmetic  12.3 us (2%)
    unnamed x5, waiting for transfers between devices  357 us
    ppermute x15, waiting for transfers between devices, body(): lax.ppermute(ring[-1], 'row', [(dev, (dev + 1) % 16) for dev in range(16)])  88.3 us
    all_gather x1, blocking collectives, body(): lax.all_gather(query_latent, 'col', axis=0, tiled=True)  47 us
    all_gather x1, blocking collectives, body(): lax.all_gather(new_rows, 'col', axis=0, tiled=True)  43.9 us
    dot_general x16, matrix products, accumulate(): jnp.einsum('qd,kd->qk', queries, key_block, preferred_element_type=jnp.fl...  18.8 us
    unnamed x66, local copies, waits for them, and re-layouts  14.7 us
  transfers between devices with their start and end apart: 18, of which 17 were waited for; matrix products, arithmetic and copies ran while one was open for 4% of the time, Pallas kernels for 0%

profile of v1, /device:TPU:16, one launch (start us, length us, event | category | flops | bytes accessed | tf_op | source)
XLA Modules:
  0.0 618.2 jit_solution(9066850102167750559)
XLA Ops:
  6.6 11.5 %collective-permute-done = bf16[1,256,288]{1,2,0:T(8,128)(2,1)S(1)} collective-permute-done((bf16[1,256,288]{1,2,0:T(8,128)(2,1)}, bf16[1,256,288]{1,2,0:T(8,128)(2,1)S(1)}, u32[]{:S(2)}, u32[]{:S(2)}) %collective-permute-start) | collective-permute-done | bytes 147488 | tf_op jit(solution)/shard_map/ppermute | solution.py:86
  18.1 5.8 collective-permute-done.1
  23.9 5.8 collective-permute-done.2
  29.6 5.8 collective-permute-done.3
  35.4 5.8 collective-permute-done.4
  41.2 5.8 collective-permute-done.5
  47.0 5.8 collective-permute-done.6
  52.8 5.8 collective-permute-done.7
  58.5 5.8 collective-permute-done.8
  65.0 5.8 collective-permute-done.9
  71.4 5.8 collective-permute-done.10
  77.9 5.8 collective-permute-done.11
  84.3 5.8 collective-permute-done.12
  90.7 5.9 collective-permute-done.13
  96.6 2.3 fusion.52
  99.1 1.4 dynamic_slice.41
  101.2 1.6 collective-permute-done.14
  111.6 1.2 select_reduce_fusion
  118.6 1.2 dynamic-slice
  121.8 136.7 %all-reduce.3.cloned.1.call-done = f32[256,1056]{1,0:T(8,128)} async-done(((f32[256,1056]{1,0:T(8,128)}), f32[256,1056]{1,0:T(8,128)}) %all-reduce.3.cloned.1.call-update) | async-done | bytes 1081360
  261.1 43.9 %all_gather.10 = bf16[256,288]{1,0:T(8,128)(2,1)S(1)} all-gather(bf16[8,288]{1,0:T(8,128)(2,1)S(1)} %pad_maximum_fusion.2), channel_id=1, replica_groups=mesh['row'=16,'col'=32] {'col'}, dimensions={0}, use_global_device_ids=true | all-gather | bytes 152064 | tf_op jit(solution)/shard_map/all_gather | solution.py:105
  307.1 47.0 %all_gather.9 = bf16[256,768]{1,0:T(8,128)(2,1)S(1)} all-gather(bf16[8,768]{1,0:T(8,128)(2,1)S(1)} %multiply_convert_fusion), channel_id=1, replica_groups=mesh['row'=16,'col'=32] {'col'}, dimensions={0}, use_global_device_ids=true | all-gather | bytes 405504 | tf_op jit(solution)/shard_map/all_gather | solution.py:74
  354.1 1.2 fusion.53
  356.1 3.0 convolution_convert_fusion
  360.1 1.3 pad_maximum_fusion
  361.4 26.9 %while.17 = (s32[]{:T(128)}, f32[256]{0:T(256)S(1)}, f32[256]{0:T(256)S(1)}, f32[256,64]{0,1:T(8,128)S(1)}, pred[8192]{0:T(1024)(128)(4,1)S(1)}, /*index=5*/bf16...) while((s32[]{:T(128)}, f32[256]{0:T(256)S(1)}, ...), condition=%wide.region_10.11_spmd, body=%wide.region_7.10_spmd.sunk | while | flops 42893828 | bytes 1935023 | solution.py:161
  368.2 1.2 fusion.68
  371.6 1.2 fusion.68
  374.9 1.2 fusion.68
  388.3 1.5 fusion.10
  389.8 1.4 copy.43
  391.3 220.3 %reduce-scatter.4.cloned.1.call-done = bf16[80,256]{1,0:T(8,128)(2,1)} async-done(((bf16[2560,256]{1,0:T(8,128)(2,1)}), bf16[80,256]{1,0:T(8,128)(2,1)}) %reduce-scatter.4.cloned.1.call-update) | async-done | bytes 40976
  (229 shorter events, 46.2 us)
Async XLA Ops:
  6.5 298.5 %copy-start = (bf16[256,4096]{1,0:T(8,128)(2,1)S(1)}, bf16[256,4096]{1,0:T(8,128)(2,1)}, u32[]{:S(2)}) copy-start(bf16[256,4096]{1,0:T(8,128)(2,1)} %param.19) | copy-start | bytes 6291460
  6.5 102.9 %copy-start.1 = (bf16[1,256,288]{1,2,0:T(8,128)(2,1)S(1)}, bf16[1,256,288]{1,2,0:T(8,128)(2,1)}, u32[]{:S(2)}) copy-start(bf16[1,256,288]{1,2,0:T(8,128)(2,1)} %param.21) | copy-start | bytes 442372
  6.5 252.0 %all-reduce.3.cloned.1.call-start = ((), (), s32[]{:S(2)}) async-start(), calls=%async_computation.3 | async-start | bytes 2359296
  6.5 11.5 %collective-permute-start = (bf16[1,256,288]{1,2,0:T(8,128)(2,1)}, bf16[1,256,288]{1,2,0:T(8,128)(2,1)S(1)}, u32[]{:S(2)}, u32[]{:S(2)}) collective-permute-start(bf16[1,256,288]{1,2,0:T(8,128)(2,1)} %param.21), channel_id=1, source_target_pairs={{0,32},{32,64},{64,96},{96,128},{128,160},{160,192},{192,224},{224... | collective-permute-start | bytes 442376 | tf_op jit(solution)/shard_map/ppermute | solution.py:86
  18.1 5.8 collective-permute-start.1
  23.9 5.8 collective-permute-start.2
  29.6 5.8 collective-permute-start.3
  35.4 5.8 collective-permute-start.4
  41.2 5.8 collective-permute-start.5
  47.0 5.8 collective-permute-start.6
  52.8 5.8 collective-permute-start.7
  58.5 5.8 collective-permute-start.8
  65.0 5.8 collective-permute-start.9
  70.8 0.7 copy-start.4
  71.4 5.8 collective-permute-start.10
  77.9 5.8 collective-permute-start.11
  84.3 5.8 collective-permute-start.12
  90.1 0.7 copy-start.10
  90.7 5.9 collective-permute-start.13
  96.6 6.1 collective-permute-start.14
  99.0 257.1 %all-gather.2.cloned.1.call-start = ((), (), s32[]{:S(2)}) async-start(), calls=%async_computation.1 | async-start | bytes 4866048 | tf_op jit(solution)/shard_map/all_gather | solution.py:104
  99.0 12.2 %copy-start.11 = (bf16[1,256,288]{1,2,0:T(8,128)(2,1)S(1)}, bf16[1,256,288]{1,2,0:T(8,128)(2,1)}, u32[]{:S(2)}) copy-start(bf16[1,256,288]{1,2,0:T(8,128)(2,1)} %copy-done.10) | copy-start | bytes 442372
  99.1 12.2 %copy-start.9 = (bf16[1,256,288]{1,2,0:T(8,128)(2,1)S(1)}, bf16[1,256,288]{1,2,0:T(8,128)(2,1)}, u32[]{:S(2)}) copy-start(bf16[1,256,288]{1,2,0:T(8,128)(2,1)} %copy-done.8) | copy-start | bytes 442372
  99.1 12.3 %copy-start.7 = (bf16[1,256,288]{1,2,0:T(8,128)(2,1)S(1)}, bf16[1,256,288]{1,2,0:T(8,128)(2,1)}, u32[]{:S(2)}) copy-start(bf16[1,256,288]{1,2,0:T(8,128)(2,1)} %copy-done.6) | copy-start | bytes 442372
  99.1 12.3 %copy-start.5 = (bf16[1,256,288]{1,2,0:T(8,128)(2,1)S(1)}, bf16[1,256,288]{1,2,0:T(8,128)(2,1)}, u32[]{:S(2)}) copy-start(bf16[1,256,288]{1,2,0:T(8,128)(2,1)} %copy-done.4) | copy-start | bytes 442372
  99.1 12.3 %copy-start.3 = (bf16[1,256,288]{1,2,0:T(8,128)(2,1)S(1)}, bf16[1,256,288]{1,2,0:T(8,128)(2,1)}, u32[]{:S(2)}) copy-start(bf16[1,256,288]{1,2,0:T(8,128)(2,1)} %copy-done.2) | copy-start | bytes 442372
  109.2 5.0 copy-start.14
  109.2 6.3 %copy-start.15 = (s32[16]{0:T(128)S(1)}, s32[16]{0:T(128)}, u32[]{:S(2)}) copy-start(s32[16]{0:T(128)} %param.22) | copy-start | bytes 196
  109.3 151.0 %copy-start.13 = (f32[256]{0:T(256)S(1)}, f32[256]{0:T(256)}, u32[]{:S(2)}) copy-start(f32[256]{0:T(256)} %param.17) | copy-start | bytes 3076
  109.3 196.9 %copy-start.12 = (f32[768]{0:T(1024)S(1)}, f32[768]{0:T(1024)}, u32[]{:S(2)}) copy-start(f32[768]{0:T(1024)} %param.16) | copy-start | bytes 9220
  112.8 498.8 %reduce-scatter.4.cloned.1.call-start = ((), (), s32[]{:S(2)}) async-start(), calls=%async_computation.2 | async-start | bytes 1351680
  359.0 1.0 slice-start
  (3 other events, 2.0 us)
Sparse Core Ops, SparseCore 0:
  99.1 159.3 all-reduce.2
  261.5 89.9 all-gather.1
  391.4 220.1 reduce-scatter.3
